TPU v7x, 512 devices: a whole 4x8x8 slice. The times are simulated.
512 devices in a mesh: vocab: 64 (over y, z_hi, core), width: 8 (over z_lo, x).
Axes of the slice: x: 4, y: 8, z: 8 (z_hi: 4, z_lo: 2; z = z_hi * 2 + z_lo), core: 2. Of those that a mesh axis runs over, the one named last changes fastest.
Arguments:
- head_weight: bfloat16 [4096, 65536], P('width', 'vocab'), may hold values from -3 to 3
- direction: bfloat16 [4096, 65536], P('width', 'vocab'), may hold values from -150 to 150
- residual: bfloat16 [4096, 65536], P('width', 'vocab'), may hold values from -150 to 150
- hidden: bfloat16 [512, 4096], P('vocab', 'width'), may hold values from -200 to 200
- fold_ids: int32 [512], replicated, may hold values from 0 to 7
Outputs:
- new_direction: bfloat16 [4096, 65536], P('width', 'vocab')
All inputs are finite; a program needn't handle non-finite values.
Results may differ from a plain program's by a relative error of at most 0.0085.
Values may be sent and summed in bfloat16 or wider, within the bound.
A program may use at most 64 MiB of HBM per device.

v0:
```python
import jax
import jax.numpy as jnp
from jax import lax
from jax.sharding import PartitionSpec as P

DAMPING = 0.02
CONTRACT_LEAD = (((0,), (1,)), ((), ()))


def local(head_weight, direction, residual, hidden, fold_ids):
    wide_panel = lax.all_gather(hidden, "width", axis=1, tiled=True)
    panels = lax.all_gather(wide_panel, "vocab", axis=0, tiled=True)
    weight_cols, direction_cols = (
        lax.all_to_all(head_weight, "width", split_axis=1, concat_axis=0, tiled=True),
        lax.all_to_all(direction, "width", split_axis=1, concat_axis=0, tiled=True),
    )
    logit_rows = lax.dot_general(
        weight_cols, panels, CONTRACT_LEAD, preferred_element_type=jnp.float32
    )
    tangent_rows = lax.dot_general(
        direction_cols, panels, CONTRACT_LEAD, preferred_element_type=jnp.float32
    )
    local_top = jnp.max(logit_rows, axis=0)
    row_top = lax.pmax(local_top, ("vocab", "width"))
    weights = jnp.exp(logit_rows - row_top[None, :])
    row_total, row_moment = lax.psum(
        (jnp.sum(weights, axis=0), jnp.sum(weights * tangent_rows, axis=0)), ("vocab", "width")
    )
    kept_mask = (fold_ids != 0).astype(jnp.float32)
    row_mean = row_moment / row_total
    curving = (
        kept_mask[None, :] * (weights / row_total[None, :]) * (tangent_rows - row_mean[None, :])
    ).astype(jnp.bfloat16)
    column_block = lax.dot_general(
        panels, curving, CONTRACT_LEAD, preferred_element_type=jnp.float32
    )
    curvature = lax.all_to_all(column_block, "width", split_axis=0, concat_axis=1, tiled=True)
    direction_wide = direction.astype(jnp.float32)
    residual_wide = residual.astype(jnp.float32)
    operator_image = curvature + DAMPING * direction_wide
    squares, curvature_sum = lax.psum(
        (jnp.sum(residual_wide * residual_wide), jnp.sum(direction_wide * operator_image)),
        ("vocab", "width"),
    )
    step_size = squares / curvature_sum
    moved = residual_wide - step_size * operator_image
    next_squares = lax.psum(jnp.sum(moved * moved), ("vocab", "width"))
    mixing = next_squares / squares
    return (moved + mixing * direction_wide).astype(jnp.bfloat16)


def solution(mesh):
    placed = (
        P("width", "vocab"),
        P("width", "vocab"),
        P("width", "vocab"),
        P("vocab", "width"),
        P(),
    )
    return jax.shard_map(
        local, mesh=mesh, in_specs=placed, out_specs=P("width", "vocab"), check_vma=False
    )
```

profile of v0, /device:TPU:1, one launch (start us, length us, event | category | flops | bytes accessed | tf_op | source)
XLA Modules:
  0.0 570.6 jit_solution(6129876579250119001)
XLA Ops:
  6.5 0.0 all-gather.2.cloned.1.call-start
  6.5 26.3 %all_gather.6 = bf16[8,4096]{1,0:T(8,128)(2,1)} all-gather(bf16[8,512]{1,0:T(8,128)(2,1)} %param.8), channel_id=1, replica_groups=mesh['vocab'=64,'width'=8] {'width'}, dimensions={1}, use_global_device_ids=true | all-gather | bytes 73728 | tf_op jit(solution)/shard_map/all_gather | solution.py:11
  32.8 0.0 all-gather.2.cloned.1.call-update
  32.8 0.0 copy-start
  32.9 2.4 copy.13
  35.2 4.1 all-to-all-start
  39.3 0.0 copy-done
  39.3 0.0 copy-start.1
  39.4 1.3 copy.15
  40.7 8.1 %all-to-all-done = bf16[512,8,128]{0,2,1:T(8,128)(2,1)S(1)} async-done(((bf16[512,8,128]{0,2,1:T(8,128)(2,1)}), bf16[512,8,128]{0,2,1:T(8,128)(2,1)S(1)}, u32[]{:S(2)}, u32[]{:S(2)}) %all-to-all-start) | async-done | bytes 1048608 | tf_op jit(solution)/shard_map/all_to_all | solution.py:14
  48.8 4.2 all-to-all-start.1
  53.0 0.0 copy-done.1
  53.1 0.7 copy.14
  53.7 11.8 %all-to-all-done.1 = bf16[512,8,128]{0,2,1:T(8,128)(2,1)} async-done(((bf16[512,8,128]{0,2,1:T(8,128)(2,1)}), bf16[512,8,128]{0,2,1:T(8,128)(2,1)}, u32[]{:S(2)}, u32[]{:S(2)}) %all-to-all-start.1) | async-done | bytes 1048608 | tf_op jit(solution)/shard_map/all_to_all | solution.py:15
  65.5 1.6 copy.16
  67.2 64.0 %all-gather.2.cloned.1.call-done = bf16[512,4096]{1,0:T(8,128)(2,1)} async-done(((bf16[8,4096]{1,0:T(8,128)(2,1)}), bf16[512,4096]{1,0:T(8,128)(2,1)}) %all-gather.2.cloned.1.call-update) | async-done | bytes 4194320 | tf_op jit(solution)/shard_map/all_gather | solution.py:12
  131.1 3.7 fusion.11
  134.8 96.2 %pmax.7 = f32[512]{0:T(512)S(1)} all-reduce(f32[512]{0:T(512)S(1)} %get-tuple-element.11), channel_id=1, replica_groups=mesh['vocab'=64,'width'=8] {'vocab','width'}, use_global_device_ids=true, to_apply=%region_3.0 | all-reduce | flops 512 | bytes 4096 | tf_op jit(solution)/shard_map/pmax | solution.py:24
  231.0 3.7 fusion.5
  234.7 93.4 %all-reduce.1 = (f32[512]{0:T(512)S(1)}, f32[512]{0:T(512)S(1)}) all-reduce(f32[512]{0:T(512)S(1)} %get-tuple-element.6, f32[512]{0:T(512)S(1)} %get-tuple-element.5), channel_id=1, replica_groups=mesh['vocab'=64,'width'=8] {'vocab','width'}, use_global_device_ids=true, to_apply=%region_7.0 | all-reduce | flops 1024 | bytes 8192 | tf_op jit(solution)/shard_map/psum | solution.py:26
  328.1 2.9 fusion.6
  331.1 0.2 copy.21
  331.3 29.6 %all_to_all.57 = f32[8,512,128]{1,2,0:T(8,128)} all-to-all(f32[8,512,128]{1,2,0:T(8,128)S(1)} %bitcast.19), channel_id=1, replica_groups=mesh['vocab'=64,'width'=8] {'width'}, dimensions={0} | all-to-all | bytes 4194304 | tf_op jit(solution)/shard_map/all_to_all | solution.py:37
  360.9 1.9 copy.18
  362.8 2.5 fusion
  365.3 95.9 %all-reduce = (f32[]{:T(128)}, f32[]{:T(128)}) all-reduce(f32[]{:T(128)} %get-tuple-element.14, f32[]{:T(128)} %get-tuple-element.15), channel_id=1, replica_groups=mesh['vocab'=64,'width'=8] {'vocab','width'}, use_global_device_ids=true, to_apply=%region_1.0 | all-reduce | flops 2 | bytes 16 | tf_op jit(solution)/shard_map/psum | solution.py:41
  462.4 2.5 multiply_reduce_fusion
  464.9 94.6 %psum.39 = f32[]{:T(128)} all-reduce(f32[]{:T(128)} %multiply_reduce_fusion), channel_id=1, replica_groups=mesh['vocab'=64,'width'=8] {'vocab','width'}, use_global_device_ids=true, to_apply=%region_11.0 | all-reduce | flops 1 | bytes 8 | tf_op jit(solution)/shard_map/psum | solution.py:47
  560.9 2.8 fusion.4
  (2 shorter events, 0.0 us)
Async XLA Ops:
  6.5 124.6 %all-gather.2.cloned.1.call-start = ((), (), s32[]{:S(2)}) async-start(), calls=%async_computation.3 | async-start | bytes 4259840 | tf_op jit(solution)/shard_map/all_gather | solution.py:12
  32.8 6.5 %copy-start = (bf16[512,1024]{1,0:T(8,128)(2,1)S(1)}, bf16[512,1024]{1,0:T(8,128)(2,1)}, u32[]{:S(2)}) copy-start(bf16[512,1024]{1,0:T(8,128)(2,1)} %param.6) | copy-start | bytes 3145732
  35.2 13.6 %all-to-all-start = ((bf16[512,8,128]{0,2,1:T(8,128)(2,1)}), bf16[512,8,128]{0,2,1:T(8,128)(2,1)S(1)}, u32[]{:S(2)}, u32[]{:S(2)}) async-start(bf16[512,8,128]{0,2,1:T(8,128)(2,1)} %bitcast), calls=%async_computation | async-start | bytes 2097152 | tf_op jit(solution)/shard_map/all_to_all | solution.py:14
  39.3 13.7 %copy-start.1 = (s32[512]{0:T(512)S(1)}, s32[512]{0:T(512)}, u32[]{:S(2)}) copy-start(s32[512]{0:T(512)} %param.9) | copy-start | bytes 6148
  48.8 16.8 %all-to-all-start.1 = ((bf16[512,8,128]{0,2,1:T(8,128)(2,1)}), bf16[512,8,128]{0,2,1:T(8,128)(2,1)}, u32[]{:S(2)}, u32[]{:S(2)}) async-start(bf16[512,8,128]{0,2,1:T(8,128)(2,1)} %bitcast.3), calls=%async_computation.1 | async-start | bytes 2097152 | tf_op jit(solution)/shard_map/all_to_all | solution.py:15
Sparse Core Ops, SparseCore 0:
  33.0 98.1 all-gather.1
where the time goes:
time: 571 us
  blocking collectives  436 us (76%)
  waiting for transfers between devices  83.9 us (15%)
  between operations  16.1 us (3%)
  matrix products  10.4 us (2%)
  starting transfers between devices  8.36 us (1%)
  local copies, waits for them, and re-layouts  8.15 us (1%)
  other arithmetic  7.74 us (1%)
    pmax x1, blocking collectives, local(): row_top = lax.pmax(local_top, ('vocab', 'width'))  96.2 us
    psum x1, blocking collectives, local(): lax.psum((jnp.sum(residual_wide * residual_wide), jnp.sum(direction_wide...  95.9 us
    psum x1, blocking collectives, local(): next_squares = lax.psum(jnp.sum(moved * moved), ('vocab', 'width'))  94.6 us
    psum x1, blocking collectives, local(): lax.psum((jnp.sum(weights, axis=0), jnp.sum(weights * tangent_rows, axis=...  93.4 us
    all_gather x1, waiting for transfers between devices, local(): panels = lax.all_gather(wide_panel, 'vocab', axis=0, tiled=True)  64 us
    all_to_all x1, blocking collectives, local(): lax.all_to_all(column_block, 'width', split_axis=0, concat_axis=1, tiled=...  29.6 us
    all_gather x1, blocking collectives, local(): wide_panel = lax.all_gather(hidden, 'width', axis=1, tiled=True)  26.3 us
    all_to_all x1, waiting for transfers between devices, local(): lax.all_to_all(direction, 'width', split_axis=1, concat_axis=0, tiled=True)  11.8 us
  transfers between devices with their start and end apart: 3, of which 3 were waited for; matrix products, arithmetic and copies ran while one was open for 1% of the time, Pallas kernels for 0%

commit v1 on v0

--- a/solution.py
+++ b/solution.py
@@ -8,7 +8,8 @@
 
 
 def local(head_weight, direction, residual, hidden, fold_ids):
-    wide_panel = lax.all_gather(hidden, "width", axis=1, tiled=True)
+    sent = jnp.stack([hidden] * lax.axis_size("width"))
+    wide_panel = jnp.concatenate(lax.all_to_all(sent, "width", 0, 0), axis=1)
     panels = lax.all_gather(wide_panel, "vocab", axis=0, tiled=True)
     weight_cols, direction_cols = (
         lax.all_to_all(head_weight, "width", split_axis=1, concat_axis=0, tiled=True),

time: 571 us -> 552 us (0.967)
  blocking collectives: 436 us -> 421 us
  waiting for transfers between devices: 83.9 us -> 75.2 us
    all_gather x1 -> x0, blocking collectives: 26.3 us -> none  [local(): wide_panel = lax.all_gather(hidden, 'width', axis=1, tiled=True)]
    all_to_all x0 -> x1, blocking collectives: none -> 11.7 us  [local(): wide_panel = jnp.concatenate(lax.all_to_all(sent, 'width', 0, 0), axis=1)]
    all_gather x1, waiting for transfers between devices: 64 us -> 52.4 us  [local(): panels = lax.all_gather(wide_panel, 'vocab', axis=0, tiled=True)]
where the time goes in v1:
time: 552 us; the launch traced here: 551 us
  blocking collectives  421 us (76%)
  waiting for transfers between devices  75.2 us (14%)
  between operations  16.1 us (3%)
  starting transfers between devices  11 us (2%)
  matrix products  10.4 us (2%)
  local copies, waits for them, and re-layouts  8.85 us (2%)
  other arithmetic  7.74 us (1%)
    pmax x1, blocking collectives, local(): row_top = lax.pmax(local_top, ('vocab', 'width'))  96.2 us
    psum x1, blocking collectives, local(): lax.psum((jnp.sum(residual_wide * residual_wide), jnp.sum(direction_wide...  95.9 us
    psum x1, blocking collectives, local(): next_squares = lax.psum(jnp.sum(moved * moved), ('vocab', 'width'))  94.7 us
    psum x1, blocking collectives, local(): lax.psum((jnp.sum(weights, axis=0), jnp.sum(weights * tangent_rows, axis=...  93.4 us
    all_gather x1, waiting for transfers between devices, local(): panels = lax.all_gather(wide_panel, 'vocab', axis=0, tiled=True)  52.4 us
    all_to_all x1, blocking collectives, local(): lax.all_to_all(column_block, 'width', split_axis=0, concat_axis=1, tiled=...  29.6 us
    all_to_all x1, waiting for transfers between devices, local(): lax.all_to_all(direction, 'width', split_axis=1, concat_axis=0, tiled=True)  14.4 us
    all_to_all x1, blocking collectives, local(): wide_panel = jnp.concatenate(lax.all_to_all(sent, 'width', 0, 0), axis=1)  11.7 us
  transfers between devices with their start and end apart: 3, of which 3 were waited for; matrix products, arithmetic and copies ran while one was open for 1% of the time, Pallas kernels for 0%

profile of v1, /device:TPU:1, one launch (start us, length us, event | category | flops | bytes accessed | tf_op | source)
XLA Modules:
  0.0 550.8 jit_solution(3807200322579672560)
XLA Ops:
  6.5 0.0 all-gather.2.cloned.1.call-start
  6.5 0.7 stack.2
  7.2 11.7 %all_to_all.62 = bf16[8,8,512]{2,1,0:T(8,128)(2,1)} all-to-all(bf16[8,8,512]{2,1,0:T(8,128)(2,1)S(1)} %stack.2), channel_id=1, replica_groups=mesh['vocab'=64,'width'=8] {'width'}, dimensions={0} | all-to-all | bytes 131072 | tf_op jit(solution)/shard_map/all_to_all | solution.py:12
  19.0 0.0 all-gather.2.cloned.1.call-update
  19.0 0.0 copy-start
  19.0 2.4 copy.13
  21.4 3.6 all-to-all-start
  24.9 0.0 copy-done
  25.0 0.0 copy-start.1
  25.0 1.3 copy.15
  26.3 8.4 %all-to-all-done = bf16[512,8,128]{0,2,1:T(8,128)(2,1)S(1)} async-done(((bf16[512,8,128]{0,2,1:T(8,128)(2,1)}), bf16[512,8,128]{0,2,1:T(8,128)(2,1)S(1)}, u32[]{:S(2)}, u32[]{:S(2)}) %all-to-all-start) | async-done | bytes 1048608 | tf_op jit(solution)/shard_map/all_to_all | solution.py:15
  34.7 7.5 %all-to-all-start.2 = ((bf16[512,8,128]{0,2,1:T(8,128)(2,1)}), bf16[512,8,128]{0,2,1:T(8,128)(2,1)}, u32[]{:S(2)}, u32[]{:S(2)}) async-start(bf16[512,8,128]{0,2,1:T(8,128)(2,1)} %bitcast.5), calls=%async_computation.2 | async-start | bytes 2097152 | tf_op jit(solution)/shard_map/all_to_all | solution.py:16
  42.2 0.0 copy-done.1
  42.2 0.7 copy.14
  42.9 14.4 %all-to-all-done.2 = bf16[512,8,128]{0,2,1:T(8,128)(2,1)} async-done(((bf16[512,8,128]{0,2,1:T(8,128)(2,1)}), bf16[512,8,128]{0,2,1:T(8,128)(2,1)}, u32[]{:S(2)}, u32[]{:S(2)}) %all-to-all-start.2) | async-done | bytes 1048608 | tf_op jit(solution)/shard_map/all_to_all | solution.py:16
  57.3 1.6 copy.16
  58.9 52.4 %all-gather.2.cloned.1.call-done = bf16[512,4096]{1,0:T(8,128)(2,1)} async-done(((bf16[8,4096]{1,0:T(8,128)(2,1)}), bf16[512,4096]{1,0:T(8,128)(2,1)}) %all-gather.2.cloned.1.call-update) | async-done | bytes 4194320 | tf_op jit(solution)/shard_map/all_gather | solution.py:13
  111.3 3.7 fusion.11
  115.0 96.2 %pmax.7 = f32[512]{0:T(512)S(1)} all-reduce(f32[512]{0:T(512)S(1)} %get-tuple-element.11), channel_id=1, replica_groups=mesh['vocab'=64,'width'=8] {'vocab','width'}, use_global_device_ids=true, to_apply=%region_3.0 | all-reduce | flops 512 | bytes 4096 | tf_op jit(solution)/shard_map/pmax | solution.py:25
  211.2 3.7 fusion.5
  214.9 93.4 %all-reduce.1 = (f32[512]{0:T(512)S(1)}, f32[512]{0:T(512)S(1)}) all-reduce(f32[512]{0:T(512)S(1)} %get-tuple-element.6, f32[512]{0:T(512)S(1)} %get-tuple-element.5), channel_id=1, replica_groups=mesh['vocab'=64,'width'=8] {'vocab','width'}, use_global_device_ids=true, to_apply=%region_7.0 | all-reduce | flops 1024 | bytes 8192 | tf_op jit(solution)/shard_map/psum | solution.py:27
  308.3 2.9 fusion.6
  311.3 0.2 copy.21
  311.5 29.6 %all_to_all.63 = f32[8,512,128]{1,2,0:T(8,128)} all-to-all(f32[8,512,128]{1,2,0:T(8,128)S(1)} %bitcast.22), channel_id=1, replica_groups=mesh['vocab'=64,'width'=8] {'width'}, dimensions={0} | all-to-all | bytes 4194304 | tf_op jit(solution)/shard_map/all_to_all | solution.py:38
  341.1 1.9 copy.18
  343.0 2.5 fusion
  345.5 95.9 %all-reduce = (f32[]{:T(128)}, f32[]{:T(128)}) all-reduce(f32[]{:T(128)} %get-tuple-element.14, f32[]{:T(128)} %get-tuple-element.15), channel_id=1, replica_groups=mesh['vocab'=64,'width'=8] {'vocab','width'}, use_global_device_ids=true, to_apply=%region_1.0 | all-reduce | flops 2 | bytes 16 | tf_op jit(solution)/shard_map/psum | solution.py:42
  442.6 2.5 multiply_reduce_fusion
  445.1 94.7 %psum.39 = f32[]{:T(128)} all-reduce(f32[]{:T(128)} %multiply_reduce_fusion), channel_id=1, replica_groups=mesh['vocab'=64,'width'=8] {'vocab','width'}, use_global_device_ids=true, to_apply=%region_11.0 | all-reduce | flops 1 | bytes 8 | tf_op jit(solution)/shard_map/psum | solution.py:48
  541.1 2.8 fusion.4
  (2 shorter events, 0.0 us)
Async XLA Ops:
  6.5 104.8 %all-gather.2.cloned.1.call-start = ((), (), s32[]{:S(2)}) async-start(), calls=%async_computation.4 | async-start | bytes 4259840 | tf_op jit(solution)/shard_map/all_gather | solution.py:13
  19.0 5.9 %copy-start = (bf16[512,1024]{1,0:T(8,128)(2,1)S(1)}, bf16[512,1024]{1,0:T(8,128)(2,1)}, u32[]{:S(2)}) copy-start(bf16[512,1024]{1,0:T(8,128)(2,1)} %param.6) | copy-start | bytes 3145732
  21.4 13.4 %all-to-all-start = ((bf16[512,8,128]{0,2,1:T(8,128)(2,1)}), bf16[512,8,128]{0,2,1:T(8,128)(2,1)S(1)}, u32[]{:S(2)}, u32[]{:S(2)}) async-start(bf16[512,8,128]{0,2,1:T(8,128)(2,1)} %bitcast), calls=%async_computation | async-start | bytes 2097152 | tf_op jit(solution)/shard_map/all_to_all | solution.py:15
  25.0 17.3 %copy-start.1 = (s32[512]{0:T(512)S(1)}, s32[512]{0:T(512)}, u32[]{:S(2)}) copy-start(s32[512]{0:T(512)} %param.9) | copy-start | bytes 6148
  34.7 22.6 %all-to-all-start.2 = ((bf16[512,8,128]{0,2,1:T(8,128)(2,1)}), bf16[512,8,128]{0,2,1:T(8,128)(2,1)}, u32[]{:S(2)}, u32[]{:S(2)}) async-start(bf16[512,8,128]{0,2,1:T(8,128)(2,1)} %bitcast.5), calls=%async_computation.2 | async-start | bytes 2097152 | tf_op jit(solution)/shard_map/all_to_all | solution.py:16
Sparse Core Ops, SparseCore 0:
  19.1 92.1 all-gather.1
